TPU v7x, 32 devices: a whole 2x2x4 slice. The times are simulated.
32 devices in a mesh: dp: 4 (over x, core), row: 4 (over z), col: 2 (over y).
Axes of the slice: x: 2, y: 2, z: 4, core: 2. Of those that a mesh axis runs over, the one named last changes fastest.
Arguments:
- tokens_in: bfloat16 [8192, 768], P(('dp', 'col'), 'row'), may hold values from -6 to 6
- out_cot: bfloat16 [8192, 768], P(('dp', 'col'), 'row'), may hold values from -6 to 6
- segments: int32 [16, 512], P('dp'), may hold values from 0 to 31, never falling along the last dimension, each value on 1 to 256 neighbouring positions
- norm_params: float32 [4, 768], P(None, 'row'), may hold values from -1.2 to 1.5, as said below
- qkv_weight: float32 [768, 2304], P('row', 'col'), may hold values from -0.21875 to 0.21875
- proj_weight: float32 [768, 768], P('col', 'row'), may hold values from -0.875 to 0.875
- up_weight: float32 [768, 3072], P('row', 'col'), may hold values from -0.21875 to 0.21875
- down_weight: float32 [3072, 768], P('col', 'row'), may hold values from -0.109375 to 0.109375
- norm_first: float32 [4, 768], P(None, 'row'), may hold values from -18 to 18
- norm_second: float32 [4, 768], P(None, 'row'), may hold values from 30 to 300
- qkv_first: float32 [768, 2304], P('row', 'col'), may hold values from -18 to 18
- qkv_second: float32 [768, 2304], P('row', 'col'), may hold values from 30 to 300
- proj_first: float32 [768, 768], P('col', 'row'), may hold values from -18 to 18
- proj_second: float32 [768, 768], P('col', 'row'), may hold values from 30 to 300
- up_first: float32 [768, 3072], P('row', 'col'), may hold values from -18 to 18
- up_second: float32 [768, 3072], P('row', 'col'), may hold values from 30 to 300
- down_first: float32 [3072, 768], P('col', 'row'), may hold values from -18 to 18
- down_second: float32 [3072, 768], P('col', 'row'), may hold values from 30 to 300
Outputs:
- output: bfloat16 [8192, 768], P(('dp', 'col'), 'row')
- input_grad: bfloat16 [8192, 768], P(('dp', 'col'), 'row')
- norm_grad: float32 [4, 768], P(None, 'row')
- qkv_grad: float32 [768, 2304], P('row', 'col')
- proj_grad: float32 [768, 768], P('col', 'row')
- up_grad: float32 [768, 3072], P('row', 'col')
- down_grad: float32 [3072, 768], P('col', 'row')
- norm_new: float32 [4, 768], P(None, 'row')
- qkv_new: float32 [768, 2304], P('row', 'col')
- proj_new: float32 [768, 768], P('col', 'row')
- up_new: float32 [768, 3072], P('row', 'col')
- down_new: float32 [3072, 768], P('col', 'row')
- norm_first_new: float32 [4, 768], P(None, 'row')
- norm_second_new: float32 [4, 768], P(None, 'row')
- qkv_first_new: float32 [768, 2304], P('row', 'col')
- qkv_second_new: float32 [768, 2304], P('row', 'col')
- proj_first_new: float32 [768, 768], P('col', 'row')
- proj_second_new: float32 [768, 768], P('col', 'row')
- up_first_new: float32 [768, 3072], P('row', 'col')
- up_second_new: float32 [768, 3072], P('row', 'col')
- down_first_new: float32 [3072, 768], P('col', 'row')
- down_second_new: float32 [3072, 768], P('col', 'row')
Inputs may be any that keep to these rules, and one draw needn't show every extreme that they name: `segments`: within a row the numbers never fall; no number covers more than 256 positions of a row, and one covers exactly that many. `norm_params`: rows 0 and 2 lie in 0.5 to 1.5.
All inputs are finite; a program needn't handle non-finite values.
Results may differ from a plain program's by a relative error of at most 0.0093.
Values may be sent and summed in bfloat16 or wider, within the bound.
A program may use at most 192 MiB of HBM per device.

v0:
```python
import math

import jax
import jax.numpy as jnp
from jax import lax
from jax.sharding import PartitionSpec as P

D = 768
HEAD_DIM = 64
ROT_DIM = 16
SEQ_LEN = 512
STEP = 3


norm_eps = 1e-05
rotary_base = 10000.0
learn_rate = 0.01
beta_first = 0.9
beta_second = 0.95
adam_eps = 1e-08
decay_rate = 0.1
mask_fill = -1e30
inv_sqrt_two = 0.7071067811865476
inv_sqrt_two_pi = 0.3989422804014327


def gelu_value(value):
    return 0.5 * value * (1.0 + lax.erf(value * inv_sqrt_two))


def gelu_slope(value):
    return 0.5 * (1.0 + lax.erf(value * inv_sqrt_two)) + value * inv_sqrt_two_pi * jnp.exp(
        -0.5 * value * value
    )


def positions_of(segs):
    length = segs.shape[-1]
    index = jnp.broadcast_to(jnp.arange(length, dtype=jnp.int32), segs.shape)
    starts = jnp.concatenate(
        [jnp.ones(segs.shape[:-1] + (1,), bool), segs[..., 1:] != segs[..., :-1]], -1
    )
    first = lax.cummax(jnp.where(starts, index, 0), axis=segs.ndim - 1)
    return index - first


def rotary_tables(positions):
    half = ROT_DIM // 2
    freq = rotary_base ** (-2.0 * jnp.arange(half, dtype=jnp.float32) / ROT_DIM)
    angle = positions.astype(jnp.float32)[..., None] * freq
    return (jnp.cos(angle), jnp.sin(angle))


def rotate(tensor, cosine, sine):
    half = ROT_DIM // 2
    cos_part = cosine[..., None, :]
    sin_part = sine[..., None, :]
    front = tensor[..., :half]
    back = tensor[..., half:ROT_DIM]
    return jnp.concatenate(
        [
            front * cos_part - back * sin_part,
            back * cos_part + front * sin_part,
            tensor[..., ROT_DIM:],
        ],
        -1,
    )


def rotate_back(grad, cosine, sine):
    half = ROT_DIM // 2
    cos_part = cosine[..., None, :]
    sin_part = sine[..., None, :]
    front = grad[..., :half]
    back = grad[..., half:ROT_DIM]
    return jnp.concatenate(
        [
            front * cos_part + back * sin_part,
            back * cos_part - front * sin_part,
            grad[..., ROT_DIM:],
        ],
        -1,
    )


def masked_scores(query, keys, segment):
    length = segment.shape[0]
    scores = jnp.einsum(
        "qhd,khd->hqk", query, keys, preferred_element_type=jnp.float32
    ) / math.sqrt(HEAD_DIM)
    index = jnp.arange(length, dtype=jnp.int32)
    allowed = (segment[:, None] == segment[None, :]) & (index[None, :] <= index[:, None])
    return jnp.where(allowed[None], scores, mask_fill)


def attend(query, keys, values, segment):
    scores = masked_scores(query, keys, segment)
    total = jnp.sum(jnp.exp(scores), -1, keepdims=True)
    logsum = jnp.log(total)
    weights = jnp.exp(scores - logsum).astype(jnp.bfloat16)
    mixed = jnp.einsum("hqk,khd->qhd", weights, values, preferred_element_type=jnp.float32).astype(
        jnp.bfloat16
    )
    return (mixed, logsum[..., 0])


def attend_back(query, keys, values, segment, logsum, mixed, grad_mixed):
    scores = masked_scores(query, keys, segment)
    probs = jnp.exp(scores - logsum[..., None])
    weights = probs.astype(jnp.bfloat16)
    value_grad = jnp.einsum("hqk,qhd->khd", weights, grad_mixed, preferred_element_type=jnp.float32)
    prod_grad = jnp.einsum("qhd,khd->hqk", grad_mixed, values, preferred_element_type=jnp.float32)
    delta = jnp.sum(grad_mixed.astype(jnp.float32) * mixed.astype(jnp.float32), -1).T
    score_grad = (probs * (prod_grad - delta[..., None]) / math.sqrt(HEAD_DIM)).astype(jnp.bfloat16)
    query_grad = jnp.einsum("hqk,khd->qhd", score_grad, keys, preferred_element_type=jnp.float32)
    key_grad = jnp.einsum("hqk,qhd->khd", score_grad, query, preferred_element_type=jnp.float32)
    return (query_grad, key_grad, value_grad)


def dot32(left, right):
    return jnp.dot(left, right, preferred_element_type=jnp.float32)


def dot_rows(left, right):
    return lax.dot_general(
        left, right, (((0,), (0,)), ((), ())), preferred_element_type=jnp.float32
    )


def dot_cols(left, right):
    return lax.dot_general(
        left, right, (((1,), (1,)), ((), ())), preferred_element_type=jnp.float32
    )


def adam_update(weight, first, second, grad, decay):
    first_new = beta_first * first + (1.0 - beta_first) * grad
    second_new = beta_second * second + (1.0 - beta_second) * grad * grad
    first_hat = first_new / (1.0 - beta_first**STEP)
    second_hat = second_new / (1.0 - beta_second**STEP)
    weight_new = weight - learn_rate * (
        first_hat / (jnp.sqrt(second_hat) + adam_eps) + decay * weight
    )
    return (weight_new, first_new, second_new)


def on_device(
    tokens_in,
    out_cot,
    segments,
    norm_params,
    qkv_weight,
    proj_weight,
    up_weight,
    down_weight,
    norm_first,
    norm_second,
    qkv_first,
    qkv_second,
    proj_first,
    proj_second,
    up_first,
    up_second,
    down_first,
    down_second,
):
    row_count = lax.axis_size("row")
    row_index = lax.axis_index("row")
    col_index = lax.axis_index("col")
    local_count = tokens_in.shape[0]
    heads_here = qkv_weight.shape[1] // (3 * HEAD_DIM)
    seq_count = segments.shape[0] // row_count
    x_all, cot_all = (
        lax.all_gather(tokens_in, "col", axis=0, tiled=True),
        lax.all_gather(out_cot, "col", axis=0, tiled=True),
    )
    group_count = x_all.shape[0]
    share = group_count // row_count
    xfull = x_all.astype(jnp.float32)
    sums = lax.psum((jnp.sum(xfull, 1), jnp.sum(xfull * xfull, 1)), "row")
    mean = sums[0] / D
    spread = sums[1] / D - mean * mean
    rstd = lax.rsqrt(spread + norm_eps)[:, None]
    normed = (xfull - mean[:, None]) * rstd
    first_in = (normed * norm_params[0] + norm_params[1]).astype(jnp.bfloat16)
    second_in = (normed * norm_params[2] + norm_params[3]).astype(jnp.bfloat16)
    qkv16 = qkv_weight.astype(jnp.bfloat16)
    up16 = up_weight.astype(jnp.bfloat16)
    proj_cat = jnp.concatenate(
        [proj_weight.astype(jnp.bfloat16), down_weight.astype(jnp.bfloat16)], 0
    )
    width_qkv = qkv16.shape[1]
    mixed_in = lax.psum_scatter(
        jnp.concatenate([dot32(first_in, qkv16), dot32(second_in, up16)], 1),
        "row",
        scatter_dimension=0,
        tiled=True,
    )
    qkv_own = mixed_in[:, :width_qkv]
    hidden_here = mixed_in[:, width_qkv:]
    seg_own = lax.dynamic_slice_in_dim(segments, row_index * seq_count, seq_count, 0)
    cosine, sine = rotary_tables(positions_of(seg_own))
    packed = qkv_own.reshape(seq_count, SEQ_LEN, heads_here, 3, HEAD_DIM)
    query = rotate(packed[..., 0, :], cosine, sine).astype(jnp.bfloat16)
    keys = rotate(packed[..., 1, :], cosine, sine).astype(jnp.bfloat16)
    values = packed[..., 2, :].astype(jnp.bfloat16)
    attended, logsum = lax.map(lambda item: attend(*item), (query, keys, values, seg_own))
    attn_width = heads_here * HEAD_DIM
    attn_flat = attended.reshape(share, attn_width)
    active = gelu_value(hidden_here).astype(jnp.bfloat16)
    attn_all, active_all = (
        lax.all_gather(attn_flat, "row", axis=0, tiled=True),
        lax.all_gather(active, "row", axis=0, tiled=True),
    )
    act_cat = jnp.concatenate([attn_all, active_all], 1)
    mixed_out = lax.psum_scatter(dot32(act_cat, proj_cat), "col", scatter_dimension=0, tiled=True)
    output = (tokens_in.astype(jnp.float32) + mixed_out).astype(jnp.bfloat16)
    grad_cat = dot_rows(act_cat, cot_all)
    act_grad = lax.psum_scatter(dot_cols(cot_all, proj_cat), "row", scatter_dimension=0, tiled=True)
    attended_grad = act_grad[:, :attn_width].astype(jnp.bfloat16)
    hidden_grad = (act_grad[:, attn_width:] * gelu_slope(hidden_here)).astype(jnp.bfloat16)
    grad_heads = attended_grad.reshape(seq_count, SEQ_LEN, heads_here, HEAD_DIM)
    query_grad, key_grad, value_grad = lax.map(
        lambda item: attend_back(*item),
        (query, keys, values, seg_own, logsum, attended, grad_heads),
    )
    query_grad = rotate_back(query_grad, cosine, sine)
    key_grad = rotate_back(key_grad, cosine, sine)
    packed_grad = (
        jnp.stack([query_grad, key_grad, value_grad], 3)
        .reshape(share, width_qkv)
        .astype(jnp.bfloat16)
    )
    packed_all, hidden_all = (
        lax.all_gather(packed_grad, "row", axis=0, tiled=True),
        lax.all_gather(hidden_grad, "row", axis=0, tiled=True),
    )
    qkv_grad = dot_rows(first_in, packed_all)
    up_grad = dot_rows(second_in, hidden_all)
    feature_count = first_in.shape[1]
    norm_in_grad = lax.psum(
        jnp.concatenate([dot_cols(packed_all, qkv16), dot_cols(hidden_all, up16)], 1), "col"
    )
    first_grad = norm_in_grad[:, :feature_count]
    second_grad = norm_in_grad[:, feature_count:]
    norm_part = jnp.stack(
        [
            jnp.sum(first_grad * normed, 0),
            jnp.sum(first_grad, 0),
            jnp.sum(second_grad * normed, 0),
            jnp.sum(second_grad, 0),
        ],
        0,
    )
    combined = norm_params[0] * first_grad + norm_params[2] * second_grad
    back_sums = lax.psum((jnp.sum(combined, 1), jnp.sum(combined * normed, 1)), "row")
    grad_all = cot_all.astype(jnp.float32) + rstd * (
        combined - back_sums[0][:, None] / D - normed * back_sums[1][:, None] / D
    )
    input_grad = lax.dynamic_slice_in_dim(grad_all, col_index * local_count, local_count, 0).astype(
        jnp.bfloat16
    )
    norm_grad, qkv_grad, proj_grad, up_grad, down_grad = lax.psum(
        (norm_part, qkv_grad, grad_cat[:attn_width], up_grad, grad_cat[attn_width:]), "dp"
    )
    norm_new, norm_first_new, norm_second_new = adam_update(
        norm_params, norm_first, norm_second, norm_grad, 0.0
    )
    qkv_new, qkv_first_new, qkv_second_new = adam_update(
        qkv_weight, qkv_first, qkv_second, qkv_grad, decay_rate
    )
    proj_new, proj_first_new, proj_second_new = adam_update(
        proj_weight, proj_first, proj_second, proj_grad, decay_rate
    )
    up_new, up_first_new, up_second_new = adam_update(
        up_weight, up_first, up_second, up_grad, decay_rate
    )
    down_new, down_first_new, down_second_new = adam_update(
        down_weight, down_first, down_second, down_grad, decay_rate
    )
    return (
        output,
        input_grad,
        norm_grad,
        qkv_grad,
        proj_grad,
        up_grad,
        down_grad,
        norm_new,
        qkv_new,
        proj_new,
        up_new,
        down_new,
        norm_first_new,
        norm_second_new,
        qkv_first_new,
        qkv_second_new,
        proj_first_new,
        proj_second_new,
        up_first_new,
        up_second_new,
        down_first_new,
        down_second_new,
    )


def solution(mesh):
    placed = (
        P(("dp", "col"), "row"),
        P(("dp", "col"), "row"),
        P("dp", None),
        P(None, "row"),
        P("row", "col"),
        P("col", "row"),
        P("row", "col"),
        P("col", "row"),
        P(None, "row"),
        P(None, "row"),
        P("row", "col"),
        P("row", "col"),
        P("col", "row"),
        P("col", "row"),
        P("row", "col"),
        P("row", "col"),
        P("col", "row"),
        P("col", "row"),
    )
    return jax.shard_map(
        on_device,
        mesh=mesh,
        in_specs=placed,
        out_specs=(
            P(("dp", "col"), "row"),
            P(("dp", "col"), "row"),
            P(None, "row"),
            P("row", "col"),
            P("col", "row"),
            P("row", "col"),
            P("col", "row"),
            P(None, "row"),
            P("row", "col"),
            P("col", "row"),
            P("row", "col"),
            P("col", "row"),
            P(None, "row"),
            P(None, "row"),
            P("row", "col"),
            P("row", "col"),
            P("col", "row"),
            P("col", "row"),
            P("row", "col"),
            P("row", "col"),
            P("col", "row"),
            P("col", "row"),
        ),
        check_vma=False,
    )
```

profile of v0, /device:TPU:0, one launch (start us, length us, event | category | flops | bytes accessed | tf_op | source)
XLA Modules:
  0.0 1250.0 jit_solution(12887507174771581139)
XLA Ops:
  7.3 13.2 %all_gather.21 = bf16[2048,192]{0,1:T(8,128)(2,1)S(1)} all-gather(bf16[1024,192]{0,1:T(8,128)(2,1)} %param.19), channel_id=1, replica_groups=mesh['dp'=4,'row'=4,'col'=2] {'col'}, dimensions={0}, use_global_device_ids=true | all-gather | bytes 1179648 | tf_op jit(solution)/shard_map/all_gather | solution.py:175
  22.1 7.8 convolution_bitcast_fusion
  30.9 10.9 all_gather.18
  42.0 20.0 %all-reduce.1 = (f32[2048]{0:T(1024)S(1)}, f32[2048]{0:T(1024)S(1)}) all-reduce(f32[2048]{0:T(1024)S(1)} %get-tuple-element.85, f32[2048]{0:T(1024)S(1)} %get-tuple-element.84), channel_id=1, replica_groups=mesh['dp'=4,'row'=4,'col'=2] {'row'}, use_global_device_ids=true, to_apply=%region_3.0 | all-reduce | flops 4096 | bytes 32768 | tf_op jit(solution)/shard_map/psum | solution.py:180
  62.1 1.6 fusion.50
  63.7 2.0 fusion.46
  65.7 11.2 pad_maximum_fusion
  79.3 0.9 fusion.30
  80.2 214.4 %reduce-scatter.8.cloned.1.call-done = f32[512,1920]{0,1:T(8,128)} async-done(((f32[2048,1920]{0,1:T(8,128)}), f32[512,1920]{0,1:T(8,128)}) %reduce-scatter.8.cloned.1.call-update) | async-done | bytes 3932176 | tf_op jit(solution)/shard_map/reduce_scatter | solution.py:219
  294.6 1.2 slice.212
  295.8 366.3 %reduce-scatter.4.cloned.1.call-done = f32[512,2688]{0,1:T(8,128)} async-done(((f32[2048,2688]{0,1:T(8,128)}), f32[512,2688]{0,1:T(8,128)}) %reduce-scatter.4.cloned.1.call-update) | async-done | bytes 5505040 | tf_op jit(solution)/shard_map/reduce_scatter | solution.py:193
  662.1 1.9 slice.132
  666.5 7.8 fusion.1
  674.3 4.8 multiply_reduce_fusion.3
  679.2 4.0 multiply_convert_fusion
  684.2 1.1 convolution_bitcast_fusion.1
  685.6 1.1 fusion.25
  686.8 1.1 copy.56
  688.0 4.9 fusion.9
  693.8 24.0 %all-gather.5.cloned.1.call-done = bf16[2048,384]{0,1:T(8,128)(2,1)} async-done(((bf16[512,384]{0,1:T(8,128)(2,1)}), bf16[2048,384]{0,1:T(8,128)(2,1)}) %all-gather.5.cloned.1.call-update) | async-done | bytes 1572880 | tf_op jit(solution)/shard_map/all_gather | solution.py:212
  717.8 2.8 constant_dynamic-update-slice_fusion.1
  720.6 87.5 %all-gather.9.cloned.1.call-done = bf16[2048,1152]{0,1:T(8,128)(2,1)} async-done(((bf16[512,1152]{0,1:T(8,128)(2,1)}), bf16[2048,1152]{0,1:T(8,128)(2,1)}) %all-gather.9.cloned.1.call-update) | async-done | bytes 4718608 | tf_op jit(solution)/shard_map/all_gather | solution.py:235
  808.1 5.0 fusion.65
  813.1 110.2 %all-gather.7.cloned.1.call-done = bf16[2048,1536]{0,1:T(8,128)(2,1)} async-done(((bf16[512,1536]{0,1:T(8,128)(2,1)}), bf16[2048,1536]{0,1:T(8,128)(2,1)}) %all-gather.7.cloned.1.call-update) | async-done | bytes 6291472 | tf_op jit(solution)/shard_map/all_gather | solution.py:213
  923.3 6.5 constant_dynamic-update-slice_fusion
  929.8 6.7 fusion.74
  936.5 1.2 slice.154
  938.4 99.8 %all-gather.11.cloned.1.call-done = bf16[2048,1536]{0,1:T(8,128)(2,1)} async-done(((bf16[512,1536]{0,1:T(8,128)(2,1)}), bf16[2048,1536]{0,1:T(8,128)(2,1)}) %all-gather.11.cloned.1.call-update) | async-done | bytes 6291472 | tf_op jit(solution)/shard_map/all_gather | solution.py:236
  1038.2 6.0 fusion.66
  1044.4 1.1 copy-done.3
  1045.5 3.5 fusion.48
  1049.0 4.2 fusion.44
  1053.2 2.1 pad_maximum_fusion.1
  1056.3 6.4 fusion.39
  1062.7 54.8 %all-reduce.8.cloned.1.call-done = (f32[192,1152]{1,0:T(8,128)}, f32[384,192]{0,1:T(8,128)}, f32[192,1536]{1,0:T(8,128)}, f32[1536,192]{0,1:T(8,128)}) async-done(((f32[192,1152]{1,0:T(8,128)}, f32[384,192]{0,1:T(8,128)}, f32[192,1536]{1,0:T(8,128)}, f32[1536,192]{0,1:T(8,128)}), (f32[192,1152]{1,0:T(8,128)}, f32[384,192]{0,1:T(8,128)}, f32[192,1536]{1,0:T(8,128)}, ...) | async-done | bytes 3538960 | tf_op jit(solution)/shard_map/psum | solution.py:263
  1117.6 2.2 multiply_subtract_fusion.3
  1119.8 4.5 multiply_subtract_fusion
  1124.4 2.4 multiply_subtract_fusion.1
  1127.6 1.9 multiply_subtract_fusion.2
  1129.5 76.3 %all-reduce.6.cloned.1.call-done = f32[2048,384]{0,1:T(8,128)} async-done(((f32[2048,384]{0,1:T(8,128)}), f32[2048,384]{0,1:T(8,128)}) %all-reduce.6.cloned.1.call-update) | async-done | bytes 3145744 | tf_op jit(solution)/shard_map/psum | solution.py:241
  1205.8 4.1 multiply_reduce_fusion.1
  1210.0 18.9 %all-reduce = (f32[2048]{0:T(1024)S(1)}, f32[2048]{0:T(1024)S(1)}) all-reduce(f32[2048]{0:T(1024)S(1)} %get-tuple-element.82, f32[2048]{0:T(1024)S(1)} %get-tuple-element.83), channel_id=1, replica_groups=mesh['dp'=4,'row'=4,'col'=2] {'row'}, use_global_device_ids=true, to_apply=%region_13.14 | all-reduce | flops 4096 | bytes 32768 | tf_op jit(solution)/shard_map/psum | solution.py:256
  1228.9 6.1 psum.75
  1235.6 2.1 fusion.35
  1237.7 2.1 add_convert_fusion.2
  1239.8 0.9 copy.80
  1241.4 1.0 copy.82
  1242.4 1.0 copy.83
  (162 shorter events, 14.2 us)
Async XLA Ops:
  7.2 13.2 %copy-start.7 = (f32[1536,192]{0,1:T(8,128)S(1)}, f32[1536,192]{0,1:T(8,128)}, u32[]{:S(2)}) copy-start(f32[1536,192]{0,1:T(8,128)} %param.25) | copy-start | bytes 3538948
  7.2 13.3 %copy-start.20 = (f32[384,192]{0,1:T(8,128)S(1)}, f32[384,192]{0,1:T(8,128)}, u32[]{:S(2)}) copy-start(f32[384,192]{0,1:T(8,128)} %param.23) | copy-start | bytes 884740
  7.2 287.4 %reduce-scatter.8.cloned.1.call-start = ((), (), s32[]{:S(2)}) async-start(), calls=%async_computation.7 | async-start | bytes 19660800 | tf_op jit(solution)/shard_map/reduce_scatter | solution.py:219
  20.4 9.4 copy-start.4
  29.9 32.1 %copy-start.41 = (f32[4,192]{1,0:T(4,128)S(1)}, f32[4,192]{1,0:T(4,128)}, u32[]{:S(2)}) copy-start(f32[4,192]{1,0:T(4,128)} %param.21) | copy-start | bytes 9220
  29.9 32.2 %copy-start.2 = (f32[192,1152]{1,0:T(8,128)S(1)}, f32[192,1152]{1,0:T(8,128)}, u32[]{:S(2)}) copy-start(f32[192,1152]{1,0:T(8,128)} %param.22) | copy-start | bytes 2654212
  29.9 632.2 %reduce-scatter.4.cloned.1.call-start = ((), (), s32[]{:S(2)}) async-start(), calls=%async_computation.3 | async-start | bytes 27525120 | tf_op jit(solution)/shard_map/reduce_scatter | solution.py:193
  62.0 1.7 copy-start.37
  62.0 1.7 copy-start.46
  62.0 1.7 copy-start.39
  62.0 1.7 copy-start.44
  76.9 640.9 %all-gather.5.cloned.1.call-start = ((), (), s32[]{:S(2)}) async-start(), calls=%async_computation.4 | async-start | bytes 1966080 | tf_op jit(solution)/shard_map/all_gather | solution.py:212
  664.1 1.7 copy-start.33
  679.1 128.9 %all-gather.9.cloned.1.call-start = ((), (), s32[]{:S(2)}) async-start(), calls=%async_computation.8 | async-start | bytes 5898240 | tf_op jit(solution)/shard_map/all_gather | solution.py:235
  679.2 4.0 copy-start.19
  679.2 4.0 copy-start.31
  679.2 4.0 copy-start.32
  679.2 6.3 slice-start
  683.3 2.3 slice-start.1
  687.9 235.3 %all-gather.7.cloned.1.call-start = ((), (), s32[]{:S(2)}) async-start(), calls=%async_computation.5 | async-start | bytes 7864320 | tf_op jit(solution)/shard_map/all_gather | solution.py:213
  692.9 345.3 %all-gather.11.cloned.1.call-start = ((), (), s32[]{:S(2)}) async-start(), calls=%async_computation.9 | async-start | bytes 7864320 | tf_op jit(solution)/shard_map/all_gather | solution.py:236
  693.5 114.6 %copy-start.38 = (f32[1,192]{1,0:T(1,128)S(1)}, f32[1,192]{1,0:T(1,128)}, u32[]{:S(2)}) copy-start(f32[1,192]{1,0:T(1,128)} %copy-done.37) | copy-start | bytes 2308
  693.5 114.6 %copy-start.47 = (f32[1,192]{1,0:T(1,128)S(1)}, f32[1,192]{1,0:T(1,128)}, u32[]{:S(2)}) copy-start(f32[1,192]{1,0:T(1,128)} %copy-done.46) | copy-start | bytes 2308
  693.5 424.0 %all-reduce.8.cloned.1.call-start = ((), (), s32[]{:S(2)}) async-start(), calls=%async_computation.11 | async-start | bytes 7077888 | tf_op jit(solution)/shard_map/psum | solution.py:263
  813.1 116.7 %copy-start.5 = (bf16[2048,192]{0,1:T(8,128)(2,1)S(1)}, bf16[2048,192]{0,1:T(8,128)(2,1)}, u32[]{:S(2)}) copy-start(bf16[2048,192]{0,1:T(8,128)(2,1)} %copy-done.4) | copy-start | bytes 2359300
  936.5 101.8 %copy-start.40 = (f32[1,192]{1,0:T(1,128)S(1)}, f32[1,192]{1,0:T(1,128)}, u32[]{:S(2)}) copy-start(f32[1,192]{1,0:T(1,128)} %copy-done.39) | copy-start | bytes 2308
  936.5 101.7 %copy-start.45 = (f32[1,192]{1,0:T(1,128)S(1)}, f32[1,192]{1,0:T(1,128)}, u32[]{:S(2)}) copy-start(f32[1,192]{1,0:T(1,128)} %copy-done.44) | copy-start | bytes 2308
  1044.3 4.7 copy-start.1
  1044.3 161.5 %all-reduce.6.cloned.1.call-start = ((), (), s32[]{:S(2)}) async-start(), calls=%async_computation.10 | async-start | bytes 6291456 | tf_op jit(solution)/shard_map/psum | solution.py:241
  1055.3 182.4 %reduce-scatter.6.cloned.1.call-start = ((), (), s32[]{:S(2)}) async-start(), calls=%async_computation.6 | async-start | bytes 2359296 | tf_op jit(solution)/shard_map/reduce_scatter | solution.py:216
  1062.7 54.9 %copy-start.21 = (f32[384,192]{0,1:T(8,128)S(1)}, f32[384,192]{0,1:T(8,128)}, u32[]{:S(2)}) copy-start(f32[384,192]{0,1:T(8,128)} %param.23) | copy-start | bytes 884740
  1062.7 54.9 %copy-start.28 = (f32[384,192]{0,1:T(8,128)S(1)}, f32[384,192]{0,1:T(8,128)}, u32[]{:S(2)}) copy-start(f32[384,192]{0,1:T(8,128)} %param.30) | copy-start | bytes 884740
  1117.6 2.2 copy-start.8
  1119.8 4.6 copy-start.10
  1119.8 4.6 copy-start.23
  1119.8 4.6 copy-start.24
  1124.3 2.5 copy-start.12
  1124.4 2.4 copy-start.25
  1124.4 3.3 copy-start.26
  1129.5 105.4 %copy-start.42 = (f32[4,192]{1,0:T(4,128)S(1)}, f32[4,192]{1,0:T(4,128)}, u32[]{:S(2)}) copy-start(f32[4,192]{1,0:T(4,128)} %param.21) | copy-start | bytes 9220
  1129.5 105.4 %copy-start.49 = (f32[4,192]{1,0:T(4,128)S(1)}, f32[4,192]{1,0:T(4,128)}, u32[]{:S(2)}) copy-start(f32[4,192]{1,0:T(4,128)} %param.26) | copy-start | bytes 9220
  1129.5 105.4 %copy-start.50 = (f32[4,192]{1,0:T(4,128)S(1)}, f32[4,192]{1,0:T(4,128)}, u32[]{:S(2)}) copy-start(f32[4,192]{1,0:T(4,128)} %param.27) | copy-start | bytes 9220
  1129.5 106.1 %copy-start.6 = (bf16[2048,192]{0,1:T(8,128)(2,1)S(1)}, bf16[2048,192]{0,1:T(8,128)(2,1)}, u32[]{:S(2)}) copy-start(bf16[2048,192]{0,1:T(8,128)(2,1)} %copy-done.4) | copy-start | bytes 2359300
  1210.0 27.7 %copy-start.17 = (bf16[1024,192]{0,1:T(8,128)(2,1)S(1)}, bf16[1024,192]{0,1:T(8,128)(2,1)}, u32[]{:S(2)}) copy-start(bf16[1024,192]{0,1:T(8,128)(2,1)} %param.18) | copy-start | bytes 1179652
  1235.0 4.8 copy-start.43
  1237.7 2.1 copy-start.13
  1237.7 3.0 copy-start.22
  1240.7 1.7 copy-start.9
  (14 other events, 15.5 us)
Sparse Core Ops, SparseCore 0:
  30.0 264.5 reduce-scatter.7
  297.0 365.1 reduce-scatter.3
  679.3 38.5 all-gather.4
  719.8 88.2 all-gather.8
  809.5 113.7 all-gather.6
  924.7 113.4 all-gather.10
  1044.4 73.0 all-reduce.7
  1119.9 85.9 all-reduce.5
  1208.1 26.1 reduce-scatter.5
where the time goes:
time: 1250 us
  waiting for transfers between devices  1030 us (82%)
  blocking collectives  69 us (6%)
  matrix products  62.5 us (5%)
  other arithmetic  41.8 us (3%)
  local copies, waits for them, and re-layouts  27.1 us (2%)
  between operations  14.5 us (1%)
    reduce_scatter x1, waiting for transfers between devices, on_device(): lax.psum_scatter(jnp.concatenate([dot32(first_in, qkv16), dot32(second_in...  366 us
    reduce_scatter x1, waiting for transfers between devices, on_device(): lax.psum_scatter(dot_cols(cot_all, proj_cat), 'row', scatter_dimension=0,...  214 us
    all_gather x1, waiting for transfers between devices, on_device(): lax.all_gather(active, 'row', axis=0, tiled=True)  110 us
    all_gather x1, waiting for transfers between devices, on_device(): lax.all_gather(hidden_grad, 'row', axis=0, tiled=True)  99.8 us
    all_gather x1, waiting for transfers between devices, on_device(): lax.all_gather(packed_grad, 'row', axis=0, tiled=True)  87.5 us
    psum x1, waiting for transfers between devices, on_device(): lax.psum(jnp.concatenate([dot_cols(packed_all, qkv16), dot_cols(hidden_al...  76.3 us
    psum x1, waiting for transfers between devices, on_device(): lax.psum((norm_part, qkv_grad, grad_cat[:attn_width], up_grad, grad_cat[a...  54.8 us
  transfers between devices with their start and end apart: 9, of which 8 were waited for; matrix products, arithmetic and copies ran while one was open for 7% of the time, Pallas kernels for 0%

commit v1 on v0

--- a/solution.py
+++ b/solution.py
@@ -142,6 +142,23 @@
         first_hat / (jnp.sqrt(second_hat) + adam_eps) + decay * weight
     )
     return (weight_new, first_new, second_new)
+
+
+def gather_weight(piece):
+    rows = piece.shape[0] // lax.axis_size("dp")
+    own = lax.dynamic_slice_in_dim(piece, lax.axis_index("dp") * rows, rows, 0)
+    return lax.all_gather(own, ("row", "dp"), axis=0, tiled=True)
+
+
+def reduce_weights(grads):
+    whole = jnp.concatenate([grad.astype(jnp.bfloat16) for grad in grads], 1)
+    part = lax.psum_scatter(whole, ("row", "dp"), scatter_dimension=0, tiled=True)
+    sums, start = [], 0
+    for grad in grads:
+        piece = part[:, start : start + grad.shape[1]]
+        sums.append(lax.all_gather(piece, "dp", axis=0, tiled=True).astype(jnp.float32))
+        start += grad.shape[1]
+    return sums
 
 
 def on_device(
@@ -166,59 +183,60 @@
 ):
     row_count = lax.axis_size("row")
     row_index = lax.axis_index("row")
+    col_count = lax.axis_size("col")
     col_index = lax.axis_index("col")
-    local_count = tokens_in.shape[0]
+    local_count, local_width = tokens_in.shape
     heads_here = qkv_weight.shape[1] // (3 * HEAD_DIM)
     seq_count = segments.shape[0] // row_count
-    x_all, cot_all = (
-        lax.all_gather(tokens_in, "col", axis=0, tiled=True),
-        lax.all_gather(out_cot, "col", axis=0, tiled=True),
-    )
-    group_count = x_all.shape[0]
+    group_count = local_count * col_count
     share = group_count // row_count
-    xfull = x_all.astype(jnp.float32)
-    sums = lax.psum((jnp.sum(xfull, 1), jnp.sum(xfull * xfull, 1)), "row")
-    mean = sums[0] / D
-    spread = sums[1] / D - mean * mean
-    rstd = lax.rsqrt(spread + norm_eps)[:, None]
-    normed = (xfull - mean[:, None]) * rstd
-    first_in = (normed * norm_params[0] + norm_params[1]).astype(jnp.bfloat16)
-    second_in = (normed * norm_params[2] + norm_params[3]).astype(jnp.bfloat16)
-    qkv16 = qkv_weight.astype(jnp.bfloat16)
-    up16 = up_weight.astype(jnp.bfloat16)
-    proj_cat = jnp.concatenate(
-        [proj_weight.astype(jnp.bfloat16), down_weight.astype(jnp.bfloat16)], 0
-    )
+    width = local_width * row_count
+    bf16 = jnp.bfloat16
+
+    def to_tokens(rows):
+        blocks = rows.reshape(row_count, share, local_width)
+        blocks = lax.all_to_all(blocks, "row", 0, 0, tiled=True)
+        return jnp.moveaxis(blocks, 0, 1).reshape(share, width)
+
+    x16 = to_tokens(lax.all_gather(tokens_in, "col", axis=0, tiled=True))
+    cot16 = to_tokens(lax.all_gather(out_cot, "col", axis=0, tiled=True))
+    norm_full = lax.all_gather(norm_params, "row", axis=1, tiled=True)
+    pieces = (qkv_weight, up_weight, proj_weight.T, down_weight.T)
+    all16 = gather_weight(jnp.concatenate([piece.astype(bf16) for piece in pieces], 1))
+    first_cut = qkv_weight.shape[1]
+    second_cut = first_cut + up_weight.shape[1]
+    qkv16 = all16[:, :first_cut]
+    up16 = all16[:, first_cut:second_cut]
+    out16 = all16[:, second_cut:]
+
+    xfull = x16.astype(jnp.float32)
+    mean = jnp.sum(xfull, 1, keepdims=True) / D
+    spread = jnp.sum(xfull * xfull, 1, keepdims=True) / D - mean * mean
+    rstd = lax.rsqrt(spread + norm_eps)
+    normed = (xfull - mean) * rstd
+    first_in = (normed * norm_full[0] + norm_full[1]).astype(bf16)
+    second_in = (normed * norm_full[2] + norm_full[3]).astype(bf16)
+    qkv_own = dot32(first_in, qkv16)
+    hidden_here = dot32(second_in, up16)
+
     width_qkv = qkv16.shape[1]
-    mixed_in = lax.psum_scatter(
-        jnp.concatenate([dot32(first_in, qkv16), dot32(second_in, up16)], 1),
-        "row",
-        scatter_dimension=0,
-        tiled=True,
-    )
-    qkv_own = mixed_in[:, :width_qkv]
-    hidden_here = mixed_in[:, width_qkv:]
     seg_own = lax.dynamic_slice_in_dim(segments, row_index * seq_count, seq_count, 0)
     cosine, sine = rotary_tables(positions_of(seg_own))
     packed = qkv_own.reshape(seq_count, SEQ_LEN, heads_here, 3, HEAD_DIM)
-    query = rotate(packed[..., 0, :], cosine, sine).astype(jnp.bfloat16)
-    keys = rotate(packed[..., 1, :], cosine, sine).astype(jnp.bfloat16)
-    values = packed[..., 2, :].astype(jnp.bfloat16)
+    query = rotate(packed[..., 0, :], cosine, sine).astype(bf16)
+    keys = rotate(packed[..., 1, :], cosine, sine).astype(bf16)
+    values = packed[..., 2, :].astype(bf16)
     attended, logsum = lax.map(lambda item: attend(*item), (query, keys, values, seg_own))
     attn_width = heads_here * HEAD_DIM
     attn_flat = attended.reshape(share, attn_width)
-    active = gelu_value(hidden_here).astype(jnp.bfloat16)
-    attn_all, active_all = (
-        lax.all_gather(attn_flat, "row", axis=0, tiled=True),
-        lax.all_gather(active, "row", axis=0, tiled=True),
-    )
-    act_cat = jnp.concatenate([attn_all, active_all], 1)
-    mixed_out = lax.psum_scatter(dot32(act_cat, proj_cat), "col", scatter_dimension=0, tiled=True)
-    output = (tokens_in.astype(jnp.float32) + mixed_out).astype(jnp.bfloat16)
-    grad_cat = dot_rows(act_cat, cot_all)
-    act_grad = lax.psum_scatter(dot_cols(cot_all, proj_cat), "row", scatter_dimension=0, tiled=True)
-    attended_grad = act_grad[:, :attn_width].astype(jnp.bfloat16)
-    hidden_grad = (act_grad[:, attn_width:] * gelu_slope(hidden_here)).astype(jnp.bfloat16)
+    active = gelu_value(hidden_here).astype(bf16)
+    act_cat = jnp.concatenate([attn_flat, active], 1)
+    out_part = dot_cols(act_cat, out16)
+    out_grad = dot_rows(cot16, act_cat)
+    act_grad = dot32(cot16, out16)
+    attended_grad = act_grad[:, :attn_width].astype(bf16)
+    hidden_grad = (act_grad[:, attn_width:] * gelu_slope(hidden_here)).astype(bf16)
+    up_grad = dot_rows(second_in, hidden_grad)
     grad_heads = attended_grad.reshape(seq_count, SEQ_LEN, heads_here, HEAD_DIM)
     query_grad, key_grad, value_grad = lax.map(
         lambda item: attend_back(*item),
@@ -227,22 +245,12 @@
     query_grad = rotate_back(query_grad, cosine, sine)
     key_grad = rotate_back(key_grad, cosine, sine)
     packed_grad = (
-        jnp.stack([query_grad, key_grad, value_grad], 3)
-        .reshape(share, width_qkv)
-        .astype(jnp.bfloat16)
-    )
-    packed_all, hidden_all = (
-        lax.all_gather(packed_grad, "row", axis=0, tiled=True),
-        lax.all_gather(hidden_grad, "row", axis=0, tiled=True),
-    )
-    qkv_grad = dot_rows(first_in, packed_all)
-    up_grad = dot_rows(second_in, hidden_all)
-    feature_count = first_in.shape[1]
-    norm_in_grad = lax.psum(
-        jnp.concatenate([dot_cols(packed_all, qkv16), dot_cols(hidden_all, up16)], 1), "col"
-    )
-    first_grad = norm_in_grad[:, :feature_count]
-    second_grad = norm_in_grad[:, feature_count:]
+        jnp.stack([query_grad, key_grad, value_grad], 3).reshape(share, width_qkv).astype(bf16)
+    )
+    qkv_grad = dot_rows(first_in, packed_grad)
+    qkv_grad, up_grad, out_grad = reduce_weights((qkv_grad, up_grad, out_grad))
+    first_grad = dot_cols(packed_grad, qkv16)
+    second_grad = dot_cols(hidden_grad, up16)
     norm_part = jnp.stack(
         [
             jnp.sum(first_grad * normed, 0),
@@ -252,17 +260,30 @@
         ],
         0,
     )
-    combined = norm_params[0] * first_grad + norm_params[2] * second_grad
-    back_sums = lax.psum((jnp.sum(combined, 1), jnp.sum(combined * normed, 1)), "row")
-    grad_all = cot_all.astype(jnp.float32) + rstd * (
-        combined - back_sums[0][:, None] / D - normed * back_sums[1][:, None] / D
-    )
-    input_grad = lax.dynamic_slice_in_dim(grad_all, col_index * local_count, local_count, 0).astype(
-        jnp.bfloat16
-    )
-    norm_grad, qkv_grad, proj_grad, up_grad, down_grad = lax.psum(
-        (norm_part, qkv_grad, grad_cat[:attn_width], up_grad, grad_cat[attn_width:]), "dp"
-    )
+    combined = norm_full[0] * first_grad + norm_full[2] * second_grad
+    back_first = jnp.sum(combined, 1, keepdims=True) / D
+    back_second = jnp.sum(combined * normed, 1, keepdims=True) / D
+    grad_part = rstd * (combined - back_first - normed * back_second)
+
+    def to_features(part):
+        blocks = part.astype(bf16).reshape(share, row_count, local_width)
+        blocks = lax.all_to_all(jnp.moveaxis(blocks, 1, 0), "row", 0, 0, tiled=True)
+        parts = blocks.reshape(col_count, local_count, local_width)
+        total = lax.dynamic_index_in_dim(parts, col_index, 0, keepdims=False).astype(jnp.float32)
+        for step in range(1, col_count):
+            peer = lax.rem(col_index + step, col_count)
+            sent = lax.dynamic_index_in_dim(parts, peer, 0, keepdims=False)
+            ring = [(i, (i + step) % col_count) for i in range(col_count)]
+            total = total + lax.ppermute(sent, "col", ring).astype(jnp.float32)
+        return total
+
+    output = (tokens_in.astype(jnp.float32) + to_features(out_part)).astype(bf16)
+    input_grad = (out_cot.astype(jnp.float32) + to_features(grad_part)).astype(bf16)
+    norm_grad = lax.dynamic_slice_in_dim(
+        lax.psum(norm_part, ("dp", "row", "col")), row_index * local_width, local_width, 1
+    )
+    proj_grad = out_grad[:, :attn_width].T
+    down_grad = out_grad[:, attn_width:].T
     norm_new, norm_first_new, norm_second_new = adam_update(
         norm_params, norm_first, norm_second, norm_grad, 0.0
     )

time: 1250 us -> 317 us (0.25)
  waiting for transfers between devices: 1030 us -> 21.7 us
  blocking collectives: 69 us -> 141 us
  starting transfers between devices: 1.03 us -> 21 us
  other arithmetic: 41.8 us -> 25.5 us
  matrix products: 62.5 us -> 47.2 us
  local copies, waits for them, and re-layouts: 27.1 us -> 42.1 us
    reduce_scatter x3 -> x0, waiting for transfers between devices: 581 us -> none  [the longest x1 366 us: on_device(): lax.psum_scatter(jnp.concatenate([dot32(first_in, qkv16), dot32(second_in...]
    all_gather x4 -> x1, waiting for transfers between devices: 322 us -> 0.01 us  [gather_weight(): return lax.all_gather(own, ('row', 'dp'), axis=0, tiled=True)]
    psum x2 -> x0, waiting for transfers between devices: 131 us -> none  [the longest x1 76.3 us: on_device(): lax.psum(jnp.concatenate([dot_cols(packed_all, qkv16), dot_cols(hidden_al...]
    all_gather x2 -> x6, blocking collectives: 24.1 us -> 83.4 us  [the longest x1 40.2 us: on_device(): norm_full = lax.all_gather(norm_params, 'row', axis=1, tiled=True)]
    all_to_all x0 -> x4, starting transfers between devices: none -> 16.6 us  [the longest x2 9.31 us: to_tokens(): blocks = lax.all_to_all(blocks, 'row', 0, 0, tiled=True)]
    all_to_all x0 -> x4, waiting for transfers between devices: none -> 15.9 us  [the longest x2 11.4 us: to_features(): blocks = lax.all_to_all(jnp.moveaxis(blocks, 1, 0), 'row', 0, 0, tiled=True)]
    psum x3 -> x1, blocking collectives: 44.9 us -> 57.2 us  [on_device(): lax.psum(norm_part, ('dp', 'row', 'col'))]
  transfers between devices with their start and end apart: 9 -> 8, of which waited for: 8 -> 3; matrix products, arithmetic and copies ran while one was open for 7% -> 12% of each run, Pallas kernels for 0% -> 0%
where the time goes in v1:
time: 317 us; the launch traced here: 313 us
  blocking collectives  141 us (44%)
  matrix products  47.2 us (15%)
  local copies, waits for them, and re-layouts  42.1 us (13%)
  other arithmetic  25.5 us (8%)
  waiting for transfers between devices  21.7 us (7%)
  starting transfers between devices  21 us (7%)
  between operations  15.2 us (5%)
    psum x1, blocking collectives, on_device(): lax.psum(norm_part, ('dp', 'row', 'col'))  57.2 us
    all_gather x1, blocking collectives, on_device(): norm_full = lax.all_gather(norm_params, 'row', axis=1, tiled=True)  40.2 us
    all_gather x3, blocking collectives, reduce_weights(): lax.all_gather(piece, 'dp', axis=0, tiled=True).astype(jnp.float32)  22.1 us
    unnamed x96, local copies, waits for them, and re-layouts  21 us
    all_gather x1, blocking collectives, on_device(): x16 = to_tokens(lax.all_gather(tokens_in, 'col', axis=0, tiled=True))  12.8 us
    dot_general x3, matrix products, dot32(): return jnp.dot(left, right, preferred_element_type=jnp.float32)  12.5 us
    all_to_all x2, waiting for transfers between devices, to_features(): blocks = lax.all_to_all(jnp.moveaxis(blocks, 1, 0), 'row', 0, 0, tiled=True)  11.4 us
    dot_general x3, matrix products, dot_cols(): lax.dot_general(left, right, (((1,), (1,)), ((), ())), preferred_element_...  11.3 us
  transfers between devices with their start and end apart: 8, of which 3 were waited for; matrix products, arithmetic and copies ran while one was open for 12% of the time, Pallas kernels for 0%

profile of v1, /device:TPU:0, one launch (start us, length us, event | category | flops | bytes accessed | tf_op | source)
XLA Modules:
  0.0 313.3 jit_solution(11491301340539677173)
XLA Ops:
  7.3 1.5 convert_bitcast_fusion
  10.9 12.8 %all_gather.21 = bf16[2048,192]{0,1:T(8,128)(2,1)S(1)} all-gather(bf16[1024,192]{0,1:T(8,128)(2,1)S(1)} %copy-done.13), channel_id=1, replica_groups=mesh['dp'=4,'row'=4,'col'=2] {'col'}, dimensions={0}, use_global_device_ids=true | all-gather | bytes 1179648 | tf_op jit(solution)/shard_map/all_gather | solution.py:201
  24.7 5.1 %all-to-all-start = ((bf16[4,512,192]{1,2,0:T(8,128)(2,1)}), bf16[4,512,192]{1,2,0:T(8,128)(2,1)S(1)}, u32[]{:S(2)}, u32[]{:S(2)}) async-start(bf16[4,512,192]{1,2,0:T(8,128)(2,1)} %bitcast.147), calls=%async_computation | async-start | bytes 1572864 | tf_op jit(solution)/shard_map/all_to_all | solution.py:198
  29.8 40.2 %all-gather = f32[4,192,4]{1,2,0:T(4,128)S(1)} all-gather(f32[1,192,4]{1,2,0:T(4,128)S(1)} %bitcast.167), channel_id=1, replica_groups=mesh['dp'=4,'row'=4,'col'=2] {'row'}, dimensions={0}, use_global_device_ids=true | all-gather | bytes 15360 | tf_op jit(solution)/shard_map/all_gather | solution.py:203
  71.1 8.4 %all_gather.24 = bf16[2048,192]{0,1:T(8,128)(2,1)S(1)} all-gather(bf16[1024,192]{0,1:T(8,128)(2,1)S(1)} %copy-done.11), channel_id=1, replica_groups=mesh['dp'=4,'row'=4,'col'=2] {'col'}, dimensions={0}, use_global_device_ids=true | all-gather | bytes 1179648 | tf_op jit(solution)/shard_map/all_gather | solution.py:202
  82.8 4.2 %all-to-all-start.2 = ((bf16[4,512,192]{1,2,0:T(8,128)(2,1)}), bf16[4,512,192]{1,2,0:T(8,128)(2,1)}, u32[]{:S(2)}, u32[]{:S(2)}) async-start(bf16[4,512,192]{1,2,0:T(8,128)(2,1)} %bitcast.146), calls=%async_computation.2 | async-start | bytes 1572864 | tf_op jit(solution)/shard_map/all_to_all | solution.py:198
  87.3 1.6 copy.201
  89.2 1.2 add_convert_fusion
  90.4 1.6 slice_bitcast_fusion
  92.0 2.5 copy.197
  94.5 2.7 convolution_bitcast_fusion.1
  97.2 1.4 copy-done.7
  98.7 4.5 %all-to-all-done.2 = bf16[4,512,192]{1,2,0:T(8,128)(2,1)} async-done(((bf16[4,512,192]{1,2,0:T(8,128)(2,1)}), bf16[4,512,192]{1,2,0:T(8,128)(2,1)}, u32[]{:S(2)}, u32[]{:S(2)}) %all-to-all-start.2) | async-done | bytes 786464 | tf_op jit(solution)/shard_map/all_to_all | solution.py:198
  103.2 3.9 %convolution_bitcast_fusion = f32[512,1920]{1,0:T(8,128)S(1)} fusion(bf16[512,768]{0,1:T(8,128)(2,1)} %bitcast.31, bf16[768,4608]{1,0:T(8,128)(2,1)} %all-gather.3.cloned.1.call-done), kind=kOutput, calls=%fused_computation.12 | convolution fusion | flops 1509949440 | bytes 7667712 | tf_op jit(solution)/shard_map/dot_general | solution.py:121
  107.1 1.8 copy-done.30
  109.8 7.4 %fusion.1 = f32[6,512,512]{1,2,0:T(8,128)} fusion(pred[512,512]{0,1:T(8,128)(4,1)} %fusion.38, bf16[512,6,48]{0,2,1:T(8,128)(2,1)S(1)} %get-tuple-element.202, bf16[512,6,8]{0,2,1:T(8,128)(2,1)S(1)} %get-tuple-element.193, bf16[512,6,8]{0,2,1:T(8,128)(2,1)S(1)} %get-tuple-element.194, bf16[512,6,48]{0,2,1:T(8,128)(2,1)S(1)} %get-tuple-element.201, ...), kind=kOutput, calls=%fused_computation.3 | convolution fusion | flops 415239680 | bytes 7340032 | tf_op jit(solution)/shard_map/while/body/eval_jaxpr/reduce_sum | solution.py:98
  117.2 4.3 %multiply_reduce_fusion.4 = (f32[512,6]{0,1:T(8,128)S(1)}, bf16[6,64,512]{2,1,0:T(8,128)(2,1)}) fusion(bf16[512,6,64]{0,2,1:T(8,128)(2,1)S(1)} %bitcast.152, f32[6,512,512]{1,2,0:T(8,128)} %fusion.1, f32[1,512,6,3,64]{1,4,3,2,0:T(8,128)S(1)} %copy-done.8), kind=kOutput, calls=%fused_computation.92 | convolution fusion | flops 203879424 | bytes 7483392 | tf_op jit(solution)/shard_map/while/body/eval_jaxpr/hqk,khd->qhd/dot_general | solution.py:101
  127.4 1.2 convolution_convert_fusion.2
  128.7 2.3 copy.215
  131.0 1.2 copy.202
  132.3 6.0 %fusion.9 = (bf16[512,1536]{1,0:T(8,128)(2,1)S(1)}, bf16[512,1536]{1,0:T(8,128)(2,1)}) fusion(f32[512,1920]{1,0:T(8,128)} %copy-done.30, bf16[768,4608]{1,0:T(8,128)(2,1)} %all-gather.3.cloned.1.call-done, f32[512,768]{1,0:T(8,128)S(1)} %copy-done.2, f32[768]{0:T(1024)S(1)} %copy-done.41, f32[768]{0:T(1024)S(1)} %copy-done.40, f32[512]{0:T(512)S(1)} %copy-done.34, ...), kind=kOutput, calls=%fused_computation.17 | convolution fusion | flops 1220149248 | bytes 10233856 | tf_op jit(solution)/shard_map/dot_general | solution.py:121
  138.2 1.2 copy-done.44
  139.4 3.1 %convolution_convert_fusion.1 = bf16[768,1536]{1,0:T(8,128)(2,1)} fusion(bf16[512,1536]{1,0:T(8,128)(2,1)S(1)} %get-tuple-element.175, f32[512,768]{1,0:T(8,128)S(1)} %copy-done.2, f32[768]{0:T(1024)S(1)} %copy-done.41, f32[768]{0:T(1024)S(1)} %copy-done.40, f32[512]{0:T(512)S(1)} %copy-done.34, f32[512]{0:T(512)S(1)} %copy-done.32), kind=kOutput, calls=%fused_computation.10 | convolution fusion | flops 1211105280 | bytes 5515264 | tf_op jit(solution)/shard_map/dot_general | solution.py:125
  142.6 2.8 copy.216
  145.4 3.5 %fusion.13 = bf16[768,1920]{0,1:T(8,128)(2,1)S(1)} fusion(bf16[512,768]{0,1:T(8,128)(2,1)} %bitcast.31, bf16[512,1536]{1,0:T(8,128)(2,1)} %get-tuple-element.176, bf16[512,384]{1,0:T(8,128)(2,1)S(1)} %copy.202), kind=kOutput, calls=%fused_computation.23 | convolution fusion | flops 1515356160 | bytes 5701632 | tf_op jit(solution)/shard_map/dot_general | solution.py:125
  149.0 3.4 %pad_maximum_fusion = bf16[768,4608]{0,1:T(8,128)(2,1)} fusion(bf16[768,1920]{0,1:T(8,128)(2,1)S(1)} %fusion.13, bf16[768,1536]{0,1:T(8,128)(2,1)S(1)} %copy.216, bf16[768,1152]{0,1:T(8,128)(2,1)S(1)} %copy-done.1), kind=kLoop, calls=%fused_computation.1 | loop fusion | flops 21233664 | bytes 14155776 | tf_op jit(solution)/shard_map/concatenate | solution.py:154
  152.4 10.3 %copy.228 = bf16[768,4608]{1,0:T(8,128)(2,1)} copy(bf16[768,4608]{0,1:T(8,128)(2,1)} %pad_maximum_fusion) | data formatting | bytes 14155776
  162.7 1.4 copy-done.45
  164.0 3.2 %fusion.17 = f32[512,768]{1,0:T(8,128)S(1)} fusion(bf16[512,1536]{1,0:T(8,128)(2,1)S(1)} %copy-done.45, bf16[768,4608]{1,0:T(8,128)(2,1)} %all-gather.3.cloned.1.call-done), kind=kOutput, calls=%fused_computation.28 | convolution fusion | flops 1207959552 | bytes 5505024 | tf_op jit(solution)/shard_map/dot_general | solution.py:131
  167.3 3.5 %multiply_reduce_fusion.1 = (f32[768]{0:T(1024)S(1)}, f32[512]{0:T(512)S(1)}, f32[768]{0:T(1024)S(1)}, f32[768]{0:T(1024)S(1)}, f32[512]{0:T(512)S(1)}, /*index=5*/f32[768]{0:T(1024)S(1)}, f32[512,768]{1,0:T(8,128)S(1)}) fusion(f32[512,768]{1,0:T(8,128)S(1)} %copy-done.3, f32[512]{0:T(512)S(1)} %copy-done.34, f32[512]{0:T(512)S(1)} %copy-done.32, ...), kind=kOutput, calls=%fused_computation.42 | convolution fusion | flops 911470592 | bytes 7694336 | tf_op jit(solution)/shard_map/dot_general | solution.py:131
  171.3 1.2 copy.213
  172.4 3.5 %all-to-all-start.3 = ((bf16[4,512,192]{1,2,0:T(8,128)(2,1)}), bf16[4,512,192]{1,2,0:T(8,128)(2,1)S(1)}, u32[]{:S(2)}, u32[]{:S(2)}) async-start(bf16[4,512,192]{1,2,0:T(8,128)(2,1)} %bitcast.47), calls=%async_computation.3 | async-start | bytes 1572864 | tf_op jit(solution)/shard_map/all_to_all | solution.py:270
  175.9 4.6 %fusion.27 = bf16[512,768]{1,0:T(8,128)(2,1)S(1)} fusion(bf16[768,4608]{1,0:T(8,128)(2,1)} %all-gather.3.cloned.1.call-done, bf16[512,1536]{1,0:T(8,128)(2,1)} %get-tuple-element.176, bf16[512,384]{1,0:T(8,128)(2,1)S(1)} %copy.202), kind=kOutput, calls=%fused_computation.57 | convolution fusion | flops 1514274816 | bytes 5701632 | tf_op jit(solution)/shard_map/dot_general | solution.py:131
  181.7 11.4 %all-to-all-done.3 = bf16[4,512,192]{1,2,0:T(8,128)(2,1)S(1)} async-done(((bf16[4,512,192]{1,2,0:T(8,128)(2,1)}), bf16[4,512,192]{1,2,0:T(8,128)(2,1)S(1)}, u32[]{:S(2)}, u32[]{:S(2)}) %all-to-all-start.3) | async-done | bytes 786464 | tf_op jit(solution)/shard_map/all_to_all | solution.py:270
  193.0 3.7 %all-to-all-start.1 = ((bf16[4,512,192]{1,2,0:T(8,128)(2,1)}), bf16[4,512,192]{1,2,0:T(8,128)(2,1)S(1)}, u32[]{:S(2)}, u32[]{:S(2)}) async-start(bf16[4,512,192]{1,2,0:T(8,128)(2,1)} %bitcast.29), calls=%async_computation.1 | async-start | bytes 1572864 | tf_op jit(solution)/shard_map/all_to_all | solution.py:270
  198.0 1.4 constant_dynamic-slice_fusion.2
  199.6 2.0 collective-permute-start.1
  201.6 57.2 %psum.7 = f32[4,768]{1,0:T(4,128)S(1)} all-reduce(f32[4,768]{1,0:T(4,128)S(1)} %pad_maximum_fusion.6), channel_id=1, replica_groups=mesh['dp'=4,'row'=4,'col'=2] {'dp','row','col'}, use_global_device_ids=true, to_apply=%region_12.13 | all-reduce | flops 3072 | bytes 24576 | tf_op jit(solution)/shard_map/psum | solution.py:283
  260.0 1.4 constant_dynamic-slice_fusion.3
  261.6 2.4 collective-permute-start
  264.6 2.0 fusion.43
  266.7 5.8 %collective-permute-done = bf16[1024,192]{0,1:T(8,128)(2,1)S(1)} collective-permute-done((bf16[1024,192]{0,1:T(8,128)(2,1)S(1)}, bf16[1024,192]{0,1:T(8,128)(2,1)S(1)}, u32[]{:S(2)}, u32[]{:S(2)}) %collective-permute-start) | collective-permute-done | bytes 393248 | tf_op jit(solution)/shard_map/ppermute | solution.py:277
  274.5 7.5 %all_gather.26 = bf16[192,1920]{1,0:T(8,128)(2,1)S(1)} all-gather(bf16[48,1920]{1,0:T(8,128)(2,1)S(1)} %slice.169), channel_id=1, replica_groups=mesh['dp'=4,'row'=4,'col'=2] {'dp'}, dimensions={0}, use_global_device_ids=true | all-gather | bytes 921600 | tf_op jit(solution)/shard_map/all_gather | solution.py:159
  282.1 7.8 %all_gather.27 = bf16[192,1536]{1,0:T(8,128)(2,1)S(1)} all-gather(bf16[48,1536]{1,0:T(8,128)(2,1)S(1)} %slice-done), channel_id=1, replica_groups=mesh['dp'=4,'row'=4,'col'=2] {'dp'}, dimensions={0}, use_global_device_ids=true | all-gather | bytes 737280 | tf_op jit(solution)/shard_map/all_gather | solution.py:159
  289.9 6.8 %all_gather.25 = bf16[192,1152]{1,0:T(8,128)(2,1)S(1)} all-gather(bf16[48,1152]{1,0:T(8,128)(2,1)S(1)} %slice-done.1), channel_id=1, replica_groups=mesh['dp'=4,'row'=4,'col'=2] {'dp'}, dimensions={0}, use_global_device_ids=true | all-gather | bytes 552960 | tf_op jit(solution)/shard_map/all_gather | solution.py:159
  296.8 2.6 multiply_subtract_fusion
  301.4 2.5 multiply_subtract_fusion.1
  304.1 2.0 multiply_subtract_fusion.2
  (164 shorter events, 24.0 us)
Async XLA Ops:
  7.2 1.6 copy-start.5
  7.2 83.2 %all-gather.3.cloned.1.call-start = ((), (), s32[]{:S(2)}) async-start(), calls=%async_computation.5 | async-start | bytes 7520256 | tf_op jit(solution)/shard_map/all_gather | solution.py:150
  7.3 1.8 copy-start.9
  23.7 6.0 %copy-start.37 = (f32[4,192]{1,0:T(4,128)S(1)}, f32[4,192]{1,0:T(4,128)}, u32[]{:S(2)}) copy-start(f32[4,192]{1,0:T(4,128)} %param.21) | copy-start | bytes 9220
  23.7 46.3 %copy-start.39 = (s32[4,512]{1,0:T(4,128)S(1)}, s32[4,512]{1,0:T(4,128)}, u32[]{:S(2)}) copy-start(s32[4,512]{1,0:T(4,128)} %param.20) | copy-start | bytes 24580
  23.7 47.4 %copy-start.11 = (bf16[1024,192]{0,1:T(8,128)(2,1)S(1)}, bf16[1024,192]{0,1:T(8,128)(2,1)}, u32[]{:S(2)}) copy-start(bf16[1024,192]{0,1:T(8,128)(2,1)} %param.19) | copy-start | bytes 1179652
  24.7 58.1 %all-to-all-start = ((bf16[4,512,192]{1,2,0:T(8,128)(2,1)}), bf16[4,512,192]{1,2,0:T(8,128)(2,1)S(1)}, u32[]{:S(2)}, u32[]{:S(2)}) async-start(bf16[4,512,192]{1,2,0:T(8,128)(2,1)} %bitcast.147), calls=%async_computation | async-start | bytes 1572864 | tf_op jit(solution)/shard_map/all_to_all | solution.py:198
  71.1 23.4 %copy-start.35 = (f32[768]{0:T(1024)}, f32[768]{0:T(1024)S(1)}, u32[]{:S(2)}) copy-start(f32[768]{0:T(1024)S(1)} %get-tuple-element.150) | copy-start | bytes 9220
  82.8 20.4 %all-to-all-start.2 = ((bf16[4,512,192]{1,2,0:T(8,128)(2,1)}), bf16[4,512,192]{1,2,0:T(8,128)(2,1)}, u32[]{:S(2)}, u32[]{:S(2)}) async-start(bf16[4,512,192]{1,2,0:T(8,128)(2,1)} %bitcast.146), calls=%async_computation.2 | async-start | bytes 1572864 | tf_op jit(solution)/shard_map/all_to_all | solution.py:198
  87.0 186.5 %reduce-scatter.4.cloned.1.call-start = ((), (), s32[]{:S(2)}) async-start(), calls=%async_computation.6 | async-start | bytes 7520256
  89.2 5.3 %copy-start.31 = (f32[512]{0:T(512)}, f32[512]{0:T(512)S(1)}, u32[]{:S(2)}) copy-start(f32[512]{0:T(512)S(1)} %get-tuple-element.197) | copy-start | bytes 6148
  89.2 5.3 %copy-start.33 = (f32[512]{0:T(512)}, f32[512]{0:T(512)S(1)}, u32[]{:S(2)}) copy-start(f32[512]{0:T(512)S(1)} %get-tuple-element.198) | copy-start | bytes 6148
  107.1 1.9 copy-start.30
  109.8 7.4 %copy-start.8 = (f32[1,512,6,3,64]{1,4,3,2,0:T(8,128)S(1)}, f32[1,512,6,3,64]{1,4,3,2,0:T(8,128)}, u32[]{:S(2)}) copy-start(f32[1,512,6,3,64]{1,4,3,2,0:T(8,128)} %copy-done.7) | copy-start | bytes 7077892
  117.2 4.6 %copy-start = (f32[6,512,512]{1,2,0:T(8,128)S(1)}, f32[6,512,512]{1,2,0:T(8,128)}, u32[]{:S(2)}) copy-start(f32[6,512,512]{1,2,0:T(8,128)} %fusion.1) | copy-start | bytes 18874372
  126.0 1.4 copy-start.25
  128.7 3.5 %copy-start.2 = (f32[512,768]{1,0:T(8,128)S(1)}, f32[512,768]{1,0:T(8,128)}, u32[]{:S(2)}) copy-start(f32[512,768]{1,0:T(8,128)} %copy.201) | copy-start | bytes 4718596
  128.7 3.5 %copy-start.32 = (f32[512]{0:T(512)S(1)}, f32[512]{0:T(512)}, u32[]{:S(2)}) copy-start(f32[512]{0:T(512)} %copy-done.31) | copy-start | bytes 6148
  128.7 3.5 %copy-start.34 = (f32[512]{0:T(512)S(1)}, f32[512]{0:T(512)}, u32[]{:S(2)}) copy-start(f32[512]{0:T(512)} %copy-done.33) | copy-start | bytes 6148
  128.7 3.5 %copy-start.40 = (f32[768]{0:T(1024)S(1)}, f32[768]{0:T(1024)}, u32[]{:S(2)}) copy-start(f32[768]{0:T(1024)} %get-tuple-element.152) | copy-start | bytes 9220
  128.7 3.5 %copy-start.41 = (f32[768]{0:T(1024)S(1)}, f32[768]{0:T(1024)}, u32[]{:S(2)}) copy-start(f32[768]{0:T(1024)} %get-tuple-element.151) | copy-start | bytes 9220
  145.4 3.5 %copy-start.1 = (bf16[768,1152]{0,1:T(8,128)(2,1)S(1)}, bf16[768,1152]{0,1:T(8,128)(2,1)}, u32[]{:S(2)}) copy-start(bf16[768,1152]{0,1:T(8,128)(2,1)} %copy.215) | copy-start | bytes 5308420
  164.0 3.2 %copy-start.3 = (f32[512,768]{1,0:T(8,128)S(1)}, f32[512,768]{1,0:T(8,128)}, u32[]{:S(2)}) copy-start(f32[512,768]{1,0:T(8,128)} %copy.201) | copy-start | bytes 4718596
  164.0 3.2 %copy-start.22 = (bf16[1,512,6,3,64]{1,4,3,2,0:T(8,128)(2,1)S(1)}, bf16[1,512,6,3,64]{1,4,3,2,0:T(8,128)(2,1)}, u32[]{:S(2)}) copy-start(bf16[1,512,6,3,64]{1,4,3,2,0:T(8,128)(2,1)} %copy-done.21) | copy-start | bytes 3538948
  164.0 3.2 %copy-start.36 = (f32[768]{0:T(1024)S(1)}, f32[768]{0:T(1024)}, u32[]{:S(2)}) copy-start(f32[768]{0:T(1024)} %copy-done.35) | copy-start | bytes 9220
  172.4 20.6 %all-to-all-start.3 = ((bf16[4,512,192]{1,2,0:T(8,128)(2,1)}), bf16[4,512,192]{1,2,0:T(8,128)(2,1)S(1)}, u32[]{:S(2)}, u32[]{:S(2)}) async-start(bf16[4,512,192]{1,2,0:T(8,128)(2,1)} %bitcast.47), calls=%async_computation.3 | async-start | bytes 1572864 | tf_op jit(solution)/shard_map/all_to_all | solution.py:270
  193.0 65.7 %all-to-all-start.1 = ((bf16[4,512,192]{1,2,0:T(8,128)(2,1)}), bf16[4,512,192]{1,2,0:T(8,128)(2,1)S(1)}, u32[]{:S(2)}, u32[]{:S(2)}) async-start(bf16[4,512,192]{1,2,0:T(8,128)(2,1)} %bitcast.29), calls=%async_computation.1 | async-start | bytes 1572864 | tf_op jit(solution)/shard_map/all_to_all | solution.py:270
  199.6 65.1 %collective-permute-start.1 = (bf16[1024,192]{0,1:T(8,128)(2,1)S(1)}, bf16[1024,192]{0,1:T(8,128)(2,1)}, u32[]{:S(2)}, u32[]{:S(2)}) collective-permute-start(bf16[1024,192]{0,1:T(8,128)(2,1)S(1)} %bitcast.162), channel_id=1, source_target_pairs={{0,1},{1,0},{2,3},{3,2},{4,5},{5,4},{6,7},{7,6},{8,9},{9,8},{10,11... | collective-permute-start | bytes 1179656 | tf_op jit(solution)/shard_map/ppermute | solution.py:277
  259.9 4.0 %copy-start.38 = (f32[4,192]{1,0:T(4,128)S(1)}, f32[4,192]{1,0:T(4,128)}, u32[]{:S(2)}) copy-start(f32[4,192]{1,0:T(4,128)} %param.21) | copy-start | bytes 9220
  259.9 4.0 %copy-start.42 = (f32[4,192]{1,0:T(4,128)S(1)}, f32[4,192]{1,0:T(4,128)}, u32[]{:S(2)}) copy-start(f32[4,192]{1,0:T(4,128)} %param.26) | copy-start | bytes 9220
  259.9 4.0 %copy-start.43 = (f32[4,192]{1,0:T(4,128)S(1)}, f32[4,192]{1,0:T(4,128)}, u32[]{:S(2)}) copy-start(f32[4,192]{1,0:T(4,128)} %param.27) | copy-start | bytes 9220
  260.0 4.7 %copy-start.12 = (bf16[1024,192]{0,1:T(8,128)(2,1)S(1)}, bf16[1024,192]{0,1:T(8,128)(2,1)}, u32[]{:S(2)}) copy-start(bf16[1024,192]{0,1:T(8,128)(2,1)} %param.19) | copy-start | bytes 1179652
  261.4 11.1 %copy-start.14 = (bf16[1024,192]{0,1:T(8,128)(2,1)S(1)}, bf16[1024,192]{0,1:T(8,128)(2,1)}, u32[]{:S(2)}) copy-start(bf16[1024,192]{0,1:T(8,128)(2,1)} %param.18) | copy-start | bytes 1179652
  261.6 10.9 %collective-permute-start = (bf16[1024,192]{0,1:T(8,128)(2,1)S(1)}, bf16[1024,192]{0,1:T(8,128)(2,1)S(1)}, u32[]{:S(2)}, u32[]{:S(2)}) collective-permute-start(bf16[1024,192]{0,1:T(8,128)(2,1)S(1)} %bitcast.163), channel_id=1, source_target_pairs={{0,1},{1,0},{2,3},{3,2},{4,5},{5,4},{6,7},{7,6},{8,9},{9,8},{10,11... | collective-permute-start | bytes 1179656 | tf_op jit(solution)/shard_map/ppermute | solution.py:277
  274.5 7.6 %slice-start = ((bf16[48,4608]{1,0:T(8,128)(2,1)}), bf16[48,1536]{1,0:T(8,128)(2,1)S(1)}, s32[]{:S(2)}) async-start(bf16[48,4608]{1,0:T(8,128)(2,1)} %reduce-scatter.4.cloned.1.call-done), calls=%async_computation.7 | async-start | bytes 294912 | tf_op jit(solution)/shard_map/slice | solution.py:158
  274.5 15.4 %slice-start.1 = ((bf16[48,4608]{1,0:T(8,128)(2,1)}), bf16[48,1152]{1,0:T(8,128)(2,1)S(1)}, s32[]{:S(2)}) async-start(bf16[48,4608]{1,0:T(8,128)(2,1)} %reduce-scatter.4.cloned.1.call-done), calls=%async_computation.8 | async-start | bytes 221184 | tf_op jit(solution)/shard_map/slice | solution.py:158
  282.0 14.7 %copy-start.4 = (f32[1536,192]{0,1:T(8,128)S(1)}, f32[1536,192]{0,1:T(8,128)}, u32[]{:S(2)}) copy-start(f32[1536,192]{0,1:T(8,128)} %param.25) | copy-start | bytes 3538948
  282.0 14.7 %copy-start.15 = (f32[1536,192]{0,1:T(8,128)S(1)}, f32[1536,192]{0,1:T(8,128)}, u32[]{:S(2)}) copy-start(f32[1536,192]{0,1:T(8,128)} %param.34) | copy-start | bytes 3538948
  282.0 14.7 %copy-start.16 = (f32[1536,192]{0,1:T(8,128)S(1)}, f32[1536,192]{0,1:T(8,128)}, u32[]{:S(2)}) copy-start(f32[1536,192]{0,1:T(8,128)} %param.35) | copy-start | bytes 3538948
  296.7 2.6 copy-start.20
  296.7 2.6 copy-start.26
  296.7 2.6 copy-start.27
  296.7 3.7 %copy-start.18 = (f32[192,1536]{1,0:T(8,128)S(1)}, f32[192,1536]{1,0:T(8,128)}, u32[]{:S(2)}) copy-start(f32[192,1536]{1,0:T(8,128)} %param.33) | copy-start | bytes 3538948
  299.3 1.7 copy-start.6
  299.3 2.0 copy-start.17
  301.4 2.6 copy-start.10
  301.4 2.6 copy-start.23
  301.4 2.7 copy-start.24
  (8 other events, 9.0 us)
Sparse Core Ops, SparseCore 0:
  10.9 76.4 all-gather.2
  162.8 102.5 reduce-scatter.3
